TPU v7x, 32 devices: a whole 2x2x4 slice. The times are simulated.
32 devices in a mesh: grp: 4 (over z), brick: 8 (over y, x, core).
Axes of the slice: x: 2, y: 2, z: 4, core: 2. Of those that a mesh axis runs over, the one named last changes fastest.
Arguments:
- store: bfloat16 [96, 256, 256], P(('grp', 'brick')), may hold values from -0.01171875 to 0.01171875
- crossing: int32 [32, 4], P('grp'), may hold values from 0 to 23, as said below
- phi: bfloat16 [32, 64, 16, 1024], P('grp', 'brick'), may hold values from -6 to 6
- rows_index: int32 [32, 4, 256], P(('grp', 'brick')), may hold values from 0 to 1023
- cols_index: int32 [32, 4, 256], P(('grp', 'brick')), may hold values from 0 to 1023
Outputs:
- hamiltonian: float32 [96, 256, 256], P(('grp', 'brick'))
Inputs may be any that keep to these rules, and one draw needn't show every extreme that they name: `crossing`: each row lists 4 different blocks of its group; block k of a group is held by the device with brick index k // 3 of that group. A row names at most 1 block held by one device, and exactly 1 of some device.
All inputs are finite; a program needn't handle non-finite values.
Results may differ from a plain program's by a relative error of at most 0.0029.
Values may be sent and summed in bfloat16 or wider, within the bound.
A program may use at most 128 MiB of HBM per device.

v0:
```python
import functools
import math

import jax
import jax.numpy as jnp
from jax import lax
from jax.experimental import pallas as pl
from jax.experimental.pallas import tpu as pltpu
from jax.sharding import PartitionSpec as P

GRAD_WEIGHT = 0.5
MESH = pl.DeviceIdType.MESH
NT = (((1,), (1,)), ((), ()))


def partner_of(bricks, brick, r):
    if bricks & (bricks - 1):
        return lax.rem(r - brick + bricks, bricks)
    other = brick
    for bit in range(bricks.bit_length() - 1):
        if r >> bit & 1:
            other = other + (1 << bit) * (1 - 2 * lax.rem(lax.div(brick, 1 << bit), 2))
    return other


def block_number(crossing_ref, own, whom, owner):
    number, taken = jnp.int32(0), jnp.int32(0)
    for j in range(crossing_ref.shape[0]):
        entry = crossing_ref[j, whom]
        hit = lax.div(entry, own) == owner
        number = jnp.where(hit, lax.rem(entry, own), number)
        taken = jnp.where(hit, 1, taken)
    return number, taken


def kernel(
    groups, bricks, size_z,
    crossing_ref, rows_hbm, cols_hbm, store_hbm, phi_hbm, out_ref,
    rows_ref, cols_ref, store_v, phi_v, outgoing, incoming, row_t, col_t, dens, halo, back, landed,
    load_sem, send_sem, recv_sem, halo_send, halo_recv, back_send, back_recv,
):
    group = lax.axis_index("grp")
    brick = lax.axis_index("brick")
    own, width = store_v.shape[0], store_v.shape[1]
    blocks = crossing_ref.shape[0]
    points, functions = phi_v.shape
    tall, wide = dens.shape

    load_store = pltpu.make_async_copy(store_hbm, store_v, load_sem.at[0])
    load_phi = pltpu.make_async_copy(phi_hbm, phi_v, load_sem.at[1])
    load_rows = pltpu.make_async_copy(rows_hbm, rows_ref, load_sem.at[2])
    load_cols = pltpu.make_async_copy(cols_hbm, cols_ref, load_sem.at[3])
    load_store.start()
    load_phi.start()
    load_rows.start()
    load_cols.start()

    def member(offset):
        return lax.rem(brick + (offset % bricks), bricks)

    partner = functools.partial(partner_of, bricks, brick)
    order = sorted(range(1, bricks), key=lambda r: (r == 1, r & 1, bin(r >> 1).count("1")))

    def place(dg, db):
        return (lax.rem(group + (dg % groups), groups), member(db))

    around = [(dg, db) for dg in (-1, 0, 1) for db in (-1, 0, 1) if (dg, db) != (0, 0)]
    reached = {(0, r) for r in range(1, bricks)}
    reached |= {(dg % groups, db % bricks) for dg, db in around}
    reached = sorted(reached)
    barrier = pltpu.get_barrier_semaphore()
    for dg, db in reached:
        pl.semaphore_signal(barrier, inc=1, device_id=place(dg, db), device_id_type=MESH)

    def position_of(owner):
        where, taken = jnp.int32(0), jnp.int32(0)
        for j in range(blocks):
            hit = lax.div(crossing_ref[j, brick], own) == owner
            where = jnp.where(hit, j, where)
            taken = jnp.where(hit, 1, taken)
        return where, taken

    load_store.wait()
    for r in order:
        number, _ = block_number(crossing_ref, own, partner(r), brick)
        outgoing[r] = store_v[number]
    number, _ = block_number(crossing_ref, own, brick, brick)
    incoming[0] = store_v[number]
    pl.semaphore_wait(barrier, len(reached))
    sends = []
    for r in order:
        copy = pltpu.make_async_remote_copy(
            src_ref=outgoing.at[r], dst_ref=incoming.at[r],
            send_sem=send_sem.at[r], recv_sem=recv_sem.at[r],
            device_id=(group, partner(r)), device_id_type=MESH,
        )
        copy.start()
        sends.append(copy)

    load_rows.wait()
    load_cols.wait()
    load_phi.wait()
    lane = lax.broadcasted_iota(jnp.int32, (width, 128), 1)

    def pick(index_ref, table_ref, j):
        index = jnp.broadcast_to(index_ref[0, pl.ds(j, 1), :], (128, width)).T
        onehot = jnp.concatenate(
            [
                jnp.where(index == lane + k * 128, 1.0, 0.0).astype(jnp.bfloat16)
                for k in range(functions // 128)
            ],
            axis=1,
        )
        table_ref[j] = lax.dot_general(
            onehot, phi_v[...], NT, preferred_element_type=jnp.float32
        ).astype(jnp.bfloat16)

    def tabulate(j, carry):
        pick(rows_ref, row_t, j)
        pick(cols_ref, col_t, j)
        return carry

    lax.fori_loop(0, blocks, tabulate, 0)

    density = jnp.zeros((1, points), jnp.float32)
    for n, r in enumerate([0] + order):
        where, taken = position_of(partner(r) if r else brick)
        if n:
            sends[n - 1].wait()
        product = jnp.dot(incoming[r], col_t[where], preferred_element_type=jnp.float32)
        term = jnp.sum(row_t[where].astype(jnp.float32) * product, axis=0, keepdims=True)
        density = density + jnp.where(taken == 1, term, 0.0)
    for x in range(tall):
        dens[x : x + 1, :] = density[:, x * wide : (x + 1) * wide]
    halo[1, 1] = dens[...]
    exchange = []
    for n, (dg, db) in enumerate(around):
        copy = pltpu.make_async_remote_copy(
            src_ref=dens, dst_ref=halo.at[1 - dg, 1 - db],
            send_sem=halo_send.at[n], recv_sem=halo_recv.at[n],
            device_id=place(dg, db), device_id_type=MESH,
        )
        copy.start()
        exchange.append(copy)
    for copy in exchange:
        copy.wait()

    field = jnp.concatenate(
        [jnp.concatenate([halo[i, k] for k in range(3)], axis=1) for i in range(3)], axis=0
    )
    rows, lanes = field.shape
    depth = lax.rem(lax.broadcasted_iota(jnp.int32, field.shape, 1), size_z)

    def along_x(f):
        return (pltpu.roll(f, rows - 1, 0) - pltpu.roll(f, 1, 0)) * 0.5

    def along_y(f):
        return (pltpu.roll(f, lanes - size_z, 1) - pltpu.roll(f, size_z, 1)) * 0.5

    def along_z(f):
        up = jnp.where(
            depth == size_z - 1, pltpu.roll(f, size_z - 1, 1), pltpu.roll(f, lanes - 1, 1)
        )
        down = jnp.where(depth == 0, pltpu.roll(f, lanes - size_z + 1, 1), pltpu.roll(f, 1, 1))
        return (up - down) * 0.5

    grad_x, grad_y, grad_z = along_x(field), along_y(field), along_z(field)
    sigma = grad_x * grad_x + grad_y * grad_y + grad_z * grad_z
    factor = 2.0 * GRAD_WEIGHT / (1.0 + sigma)
    diverge = along_x(factor * grad_x) + along_y(factor * grad_y) + along_z(factor * grad_z)
    centre = field[tall : 2 * tall, wide : 2 * wide]
    potential = centre / jnp.sqrt(1.0 + centre * centre) - diverge[
        tall : 2 * tall, wide : 2 * wide
    ]
    scaled = potential * (1.0 / math.sqrt(points))
    scaled = jnp.concatenate([scaled[x : x + 1, :] for x in range(tall)], axis=1)

    returns = []
    for r in order + [0]:
        where, _ = position_of(partner(r) if r else brick)
        weighted = (col_t[where].astype(jnp.float32) * scaled).astype(jnp.bfloat16)
        back[r] = lax.dot_general(
            row_t[where], weighted, NT, preferred_element_type=jnp.float32
        ).astype(jnp.bfloat16)
        if r:
            copy = pltpu.make_async_remote_copy(
                src_ref=back.at[r], dst_ref=landed.at[r],
                send_sem=back_send.at[r], recv_sem=back_recv.at[r],
                device_id=(group, partner(r)), device_id_type=MESH,
            )
            copy.start()
            returns.append(copy)
    for n, r in enumerate([0] + order):
        number, taken = block_number(crossing_ref, own, partner(r) if r else brick, brick)
        if n:
            returns[n - 1].wait()
        value = (landed if n else back)[r].astype(jnp.float32)
        for k in range(own):
            term = jnp.where((taken == 1) & (number == k), value, 0.0)
            out_ref[k] = out_ref[k] + term if n else term


def local(groups, bricks, store, crossing, phi, rows_index, cols_index):
    own, width = store.shape[0], store.shape[1]
    crossing = crossing.T
    blocks = crossing.shape[0]
    size_x, size_y, size_z, functions = phi.shape
    points = size_x * size_y * size_z
    tall, wide = size_x, size_y * size_z
    slots = (bricks, width, width)
    return pl.pallas_call(
        functools.partial(kernel, groups, bricks, size_z),
        out_shape=jax.ShapeDtypeStruct((own, width, width), jnp.float32),
        in_specs=[
            pl.BlockSpec(memory_space=pltpu.SMEM),
            pl.BlockSpec(memory_space=pl.ANY),
            pl.BlockSpec(memory_space=pl.ANY),
            pl.BlockSpec(memory_space=pl.ANY),
            pl.BlockSpec(memory_space=pl.ANY),
        ],
        out_specs=pl.BlockSpec(memory_space=pltpu.VMEM),
        scratch_shapes=[
            pltpu.VMEM(rows_index.shape, jnp.int32),
            pltpu.VMEM(cols_index.shape, jnp.int32),
            pltpu.VMEM((own, width, width), jnp.bfloat16),
            pltpu.VMEM((points, functions), jnp.bfloat16),
            pltpu.VMEM(slots, jnp.bfloat16),
            pltpu.VMEM(slots, jnp.bfloat16),
            pltpu.VMEM((blocks, width, points), jnp.bfloat16),
            pltpu.VMEM((blocks, width, points), jnp.bfloat16),
            pltpu.VMEM((tall, wide), jnp.float32),
            pltpu.VMEM((3, 3, tall, wide), jnp.float32),
            pltpu.VMEM(slots, jnp.bfloat16),
            pltpu.VMEM(slots, jnp.bfloat16),
            pltpu.SemaphoreType.DMA((4,)),
            pltpu.SemaphoreType.DMA((bricks,)),
            pltpu.SemaphoreType.DMA((bricks,)),
            pltpu.SemaphoreType.DMA((8,)),
            pltpu.SemaphoreType.DMA((8,)),
            pltpu.SemaphoreType.DMA((bricks,)),
            pltpu.SemaphoreType.DMA((bricks,)),
        ],
        compiler_params=pltpu.CompilerParams(
            collective_id=0, has_side_effects=True, vmem_limit_bytes=60 << 20
        ),
    )(crossing, rows_index, cols_index, store, phi.reshape(points, functions))


def solution(mesh):
    in_specs = (
        P(("grp", "brick"), None, None),
        P("grp", None),
        P("grp", "brick", None, None),
        P(("grp", "brick"), None, None),
        P(("grp", "brick"), None, None),
    )
    out_specs = P(("grp", "brick"), None, None)
    body = functools.partial(local, mesh.shape["grp"], mesh.shape["brick"])
    return jax.shard_map(body, mesh=mesh, in_specs=in_specs, out_specs=out_specs, check_vma=False)
```

profile of v0, /device:TPU:0, one launch (start us, length us, event | category | flops | bytes accessed | tf_op | source)
XLA Modules:
  0.0 41.2 jit_solution(6131313598048023359)
XLA Ops:
  0.0 39.1 %shard_map.55 = f32[3,256,256]{2,1,0:T(8,128)} custom-call(s32[4,8]{1,0:T(4,128)} %bitcast.3, s32[1,4,256]{2,1,0:T(4,128)} %rows_hbm.1, s32[1,4,256]{2,1,0:T(4,128)} %cols_hbm.1, bf16[3,256,256]{2,1,0:T(8,128)(2,1)} %store_hbm.1, bf16[1024,1024]{1,0:T(8,128)(2,1)} %bitcast.2), custom_call_target="tpu_custom_call" | custom-call | tf_op jit(solution)/shard_map/pallas_call | solution.py:211
  39.1 2.1 %copy.7 = f32[3,256,256]{2,1,0:T(8,128)} copy(f32[3,256,256]{2,1,0:T(8,128)} %shard_map.55) | data formatting | bytes 1572864
where the time goes:
time: 41.5 us; the launch traced here: 41.2 us
  Pallas kernels  39.1 us (94%)
  local copies, waits for them, and re-layouts  2.06 us (5%)
    pallas_call x1, Pallas kernels, local(): pl.pallas_call(functools.partial(kernel, groups, bricks, size_z), out_sha...  39.1 us
    unnamed x1, local copies, waits for them, and re-layouts  2.06 us

commit v1 on v0

--- a/solution.py
+++ b/solution.py
@@ -9,6 +9,7 @@
 from jax.sharding import PartitionSpec as P
 
 GRAD_WEIGHT = 0.5
+CORE, LOW, HIGH = 2, 2, 2
 MESH = pl.DeviceIdType.MESH
 NT = (((1,), (1,)), ((), ()))
 
@@ -31,6 +32,75 @@
         number = jnp.where(hit, lax.rem(entry, own), number)
         taken = jnp.where(hit, 1, taken)
     return number, taken
+
+
+def make_tabulate(rows_ref, cols_ref, phi_v, row_t, col_t):
+    width, functions = row_t.shape[1], phi_v.shape[1]
+    lane = lax.broadcasted_iota(jnp.int32, (width, 128), 1)
+
+    def pick(index_ref, table_ref, j):
+        index = jnp.broadcast_to(index_ref[0, pl.ds(j, 1), :], (128, width)).T
+        onehot = jnp.concatenate(
+            [
+                jnp.where(index == lane + k * 128, 1.0, 0.0).astype(jnp.bfloat16)
+                for k in range(functions // 128)
+            ],
+            axis=1,
+        )
+        table_ref[j] = lax.dot_general(
+            onehot, phi_v[...], NT, preferred_element_type=jnp.float32
+        ).astype(jnp.bfloat16)
+
+    def tabulate(j, carry):
+        pick(rows_ref, row_t, j)
+        pick(cols_ref, col_t, j)
+        return carry
+
+    return tabulate
+
+
+def scaled_potential(halo, size_z):
+    tall, wide = halo.shape[2:]
+    points = tall * wide
+    field = jnp.concatenate(
+        [jnp.concatenate([halo[i, k] for k in range(3)], axis=1) for i in range(3)], axis=0
+    )
+    rows, lanes = field.shape
+    depth = lax.rem(lax.broadcasted_iota(jnp.int32, field.shape, 1), size_z)
+
+    def along_x(f):
+        return (pltpu.roll(f, rows - 1, 0) - pltpu.roll(f, 1, 0)) * 0.5
+
+    def along_y(f):
+        return (pltpu.roll(f, lanes - size_z, 1) - pltpu.roll(f, size_z, 1)) * 0.5
+
+    def along_z(f):
+        up = jnp.where(
+            depth == size_z - 1, pltpu.roll(f, size_z - 1, 1), pltpu.roll(f, lanes - 1, 1)
+        )
+        down = jnp.where(depth == 0, pltpu.roll(f, lanes - size_z + 1, 1), pltpu.roll(f, 1, 1))
+        return (up - down) * 0.5
+
+    grad_x, grad_y, grad_z = along_x(field), along_y(field), along_z(field)
+    sigma = grad_x * grad_x + grad_y * grad_y + grad_z * grad_z
+    factor = 2.0 * GRAD_WEIGHT / (1.0 + sigma)
+    diverge = along_x(factor * grad_x) + along_y(factor * grad_y) + along_z(factor * grad_z)
+    centre = field[tall : 2 * tall, wide : 2 * wide]
+    potential = centre / jnp.sqrt(1.0 + centre * centre) - diverge[
+        tall : 2 * tall, wide : 2 * wide
+    ]
+    scaled = potential * (1.0 / math.sqrt(points))
+    scaled = jnp.concatenate([scaled[x : x + 1, :] for x in range(tall)], axis=1)
+    return scaled
+
+
+def position_in(crossing_ref, own, whom, owner):
+    where, taken = jnp.int32(0), jnp.int32(0)
+    for j in range(crossing_ref.shape[0]):
+        hit = lax.div(crossing_ref[j, whom], own) == owner
+        where = jnp.where(hit, j, where)
+        taken = jnp.where(hit, 1, taken)
+    return where, taken
 
 
 def kernel(
@@ -72,13 +142,7 @@
     for dg, db in reached:
         pl.semaphore_signal(barrier, inc=1, device_id=place(dg, db), device_id_type=MESH)
 
-    def position_of(owner):
-        where, taken = jnp.int32(0), jnp.int32(0)
-        for j in range(blocks):
-            hit = lax.div(crossing_ref[j, brick], own) == owner
-            where = jnp.where(hit, j, where)
-            taken = jnp.where(hit, 1, taken)
-        return where, taken
+    position_of = functools.partial(position_in, crossing_ref, own, brick)
 
     load_store.wait()
     for r in order:
@@ -100,26 +164,7 @@
     load_rows.wait()
     load_cols.wait()
     load_phi.wait()
-    lane = lax.broadcasted_iota(jnp.int32, (width, 128), 1)
-
-    def pick(index_ref, table_ref, j):
-        index = jnp.broadcast_to(index_ref[0, pl.ds(j, 1), :], (128, width)).T
-        onehot = jnp.concatenate(
-            [
-                jnp.where(index == lane + k * 128, 1.0, 0.0).astype(jnp.bfloat16)
-                for k in range(functions // 128)
-            ],
-            axis=1,
-        )
-        table_ref[j] = lax.dot_general(
-            onehot, phi_v[...], NT, preferred_element_type=jnp.float32
-        ).astype(jnp.bfloat16)
-
-    def tabulate(j, carry):
-        pick(rows_ref, row_t, j)
-        pick(cols_ref, col_t, j)
-        return carry
-
+    tabulate = make_tabulate(rows_ref, cols_ref, phi_v, row_t, col_t)
     lax.fori_loop(0, blocks, tabulate, 0)
 
     density = jnp.zeros((1, points), jnp.float32)
@@ -145,35 +190,7 @@
     for copy in exchange:
         copy.wait()
 
-    field = jnp.concatenate(
-        [jnp.concatenate([halo[i, k] for k in range(3)], axis=1) for i in range(3)], axis=0
-    )
-    rows, lanes = field.shape
-    depth = lax.rem(lax.broadcasted_iota(jnp.int32, field.shape, 1), size_z)
-
-    def along_x(f):
-        return (pltpu.roll(f, rows - 1, 0) - pltpu.roll(f, 1, 0)) * 0.5
-
-    def along_y(f):
-        return (pltpu.roll(f, lanes - size_z, 1) - pltpu.roll(f, size_z, 1)) * 0.5
-
-    def along_z(f):
-        up = jnp.where(
-            depth == size_z - 1, pltpu.roll(f, size_z - 1, 1), pltpu.roll(f, lanes - 1, 1)
-        )
-        down = jnp.where(depth == 0, pltpu.roll(f, lanes - size_z + 1, 1), pltpu.roll(f, 1, 1))
-        return (up - down) * 0.5
-
-    grad_x, grad_y, grad_z = along_x(field), along_y(field), along_z(field)
-    sigma = grad_x * grad_x + grad_y * grad_y + grad_z * grad_z
-    factor = 2.0 * GRAD_WEIGHT / (1.0 + sigma)
-    diverge = along_x(factor * grad_x) + along_y(factor * grad_y) + along_z(factor * grad_z)
-    centre = field[tall : 2 * tall, wide : 2 * wide]
-    potential = centre / jnp.sqrt(1.0 + centre * centre) - diverge[
-        tall : 2 * tall, wide : 2 * wide
-    ]
-    scaled = potential * (1.0 / math.sqrt(points))
-    scaled = jnp.concatenate([scaled[x : x + 1, :] for x in range(tall)], axis=1)
+    scaled = scaled_potential(halo, size_z)
 
     returns = []
     for r in order + [0]:
@@ -200,6 +217,263 @@
             out_ref[k] = out_ref[k] + term if n else term
 
 
+def cube_kernel(
+    groups, bricks, size_z,
+    crossing_ref, rows_hbm, cols_hbm, store_hbm, phi_hbm, out_ref,
+    rows_ref, cols_ref, store_v, phi_v, mate, picked, stage, incoming, row_t, col_t,
+    dens, halo, back, kept, relay, sums, direct, mate_back, sums_back,
+    load_sem, send_sem, recv_sem, ready, halo_send, halo_recv, back_send, back_recv,
+):
+    group = lax.axis_index("grp")
+    brick = lax.axis_index("brick")
+    own, width = store_v.shape[0], store_v.shape[1]
+    half = width // 2
+    points = phi_v.shape[0]
+    blocks = crossing_ref.shape[0]
+    tall, wide = dens.shape
+    upper, lower = pl.ds(0, half), pl.ds(half, half)
+    low, high = CORE, CORE * LOW
+    partner = functools.partial(partner_of, bricks, brick)
+    number_of = functools.partial(block_number, crossing_ref, own)
+
+    loads = [
+        pltpu.make_async_copy(source, target, load_sem.at[n])
+        for n, (source, target) in enumerate(
+            ((store_hbm, store_v), (rows_hbm, rows_ref), (cols_hbm, cols_ref), (phi_hbm, phi_v))
+        )
+    ]
+    barrier = pltpu.get_barrier_semaphore()
+    near = (1, low, low + 1, high, high + 1)
+
+    def along_chain(semaphore):
+        @pl.when(group > 0)
+        def _():
+            pl.semaphore_signal(
+                semaphore, inc=1, device_id=(group - 1, brick), device_id_type=MESH
+            )
+
+        @pl.when(group < groups - 1)
+        def _():
+            pl.semaphore_signal(
+                semaphore, inc=1, device_id=(group + 1, brick), device_id_type=MESH
+            )
+
+    links = jnp.where(group > 0, 1, 0) + jnp.where(group < groups - 1, 1, 0)
+    for r in near:
+        pl.semaphore_signal(barrier, inc=1, device_id=(group, partner(r)), device_id_type=MESH)
+    along_chain(barrier)
+    for load in loads:
+        load.start()
+    pl.semaphore_wait(barrier, len(near) + links)
+
+    for r in near:
+        pl.semaphore_signal(ready.at[0], inc=1, device_id=(group, partner(r)), device_id_type=MESH)
+
+    def spread(n):
+        if n >= groups:
+            return
+        pl.semaphore_wait(ready.at[n], links if n else len(near))
+        if n + 1 < groups:
+            along_chain(ready.at[n + 1])
+
+    def sender(send, recv):
+        def start(n, source, target, r):
+            copy = pltpu.make_async_remote_copy(
+                src_ref=source, dst_ref=target, send_sem=send.at[n], recv_sem=recv.at[n],
+                device_id=(group, partner(r)), device_id_type=MESH,
+            )
+            copy.start()
+            return copy
+        return start
+
+    give = sender(send_sem, recv_sem)
+    sends = {}
+    sends[0] = give(0, store_hbm.at[:, upper], stage.at[0], high)
+    sends[1] = give(1, store_hbm.at[:, lower], stage.at[1], low)
+    loads[0].wait()
+    for n, r, side in ((3, low, upper), (5, high, lower), (4, low + 1, upper), (6, high + 1, lower)):
+        number, _ = number_of(partner(r), brick)
+        picked[n - 3] = store_v[number, side]
+        sends[n] = give(n, picked.at[n - 3], incoming.at[r, side], r)
+    number, _ = number_of(partner(1), brick)
+    mate[...] = store_v[number]
+    sends[2] = give(2, mate, incoming.at[1], 1)
+    number, _ = number_of(brick, brick)
+    incoming[0] = store_v[number]
+
+    for load in loads[1:]:
+        load.wait()
+    tabulate = make_tabulate(rows_ref, cols_ref, phi_v, row_t, col_t)
+    lax.fori_loop(0, blocks, tabulate, 0)
+
+    sends[0].wait_recv()
+    sends[1].wait_recv()
+    relays = (
+        (7, low, high, upper), (9, high, low, lower),
+        (8, low + 1, high, upper), (10, high + 1, low, lower),
+        (11, 1, high, upper), (12, 1, low, lower),
+    )
+    for n, r, via, side in relays:
+        number, _ = number_of(partner(r), partner(via))
+        picked[n - 3] = stage[0 if via == high else 1, number]
+        sends[n] = give(n, picked.at[n - 3], incoming.at[r ^ via, side], r)
+    number, _ = number_of(brick, partner(high))
+    incoming[high, upper] = stage[0, number]
+    number, _ = number_of(brick, partner(low))
+    incoming[low, lower] = stage[1, number]
+
+    arrivals = (
+        (0, ()), (1, (2,)), (low, (3,)), (high, (5,)), (low + 1, (4, 12)), (high + 1, (6, 11)),
+        (low + high, (7, 9)), (low + high + 1, (8, 10)),
+    )
+    density = jnp.zeros((1, points), jnp.float32)
+    for step, (r, needs) in enumerate(arrivals):
+        where, taken = position_in(crossing_ref, own, brick, partner(r) if r else brick)
+        for n in needs:
+            sends[n].wait_recv()
+        product = jnp.dot(incoming[r], col_t[where], preferred_element_type=jnp.float32)
+        term = jnp.sum(row_t[where].astype(jnp.float32) * product, axis=0, keepdims=True)
+        density = density + jnp.where(taken == 1, term, 0.0)
+        if step < len(arrivals) - 1:
+            spread(step)
+    for n in range(len(arrivals) - 1, groups):
+        spread(n)
+    for x in range(tall):
+        dens[x : x + 1, :] = density[:, x * wide : (x + 1) * wide]
+    around = [(dg, db) for dg in (-1, 0, 1) for db in (-1, 0, 1) if (dg, db) != (0, 0)]
+    exchange = []
+    for n, (dg, db) in enumerate(around):
+        target = (lax.rem(group + dg % groups, groups), lax.rem(brick + db % bricks, bricks))
+        copy = pltpu.make_async_remote_copy(
+            src_ref=dens, dst_ref=halo.at[1 - dg, 1 - db],
+            send_sem=halo_send.at[n], recv_sem=halo_recv.at[n],
+            device_id=target, device_id_type=MESH,
+        )
+        copy.start()
+        exchange.append(copy)
+    halo[1, 1] = dens[...]
+    for n in sends:
+        sends[n].wait_send()
+    for copy in exchange:
+        copy.wait()
+    scaled = scaled_potential(halo, size_z)
+
+    def partial_of(r):
+        where, _ = position_in(crossing_ref, own, brick, partner(r) if r else brick)
+        weighted = (col_t[where].astype(jnp.float32) * scaled).astype(jnp.bfloat16)
+        return lax.dot_general(row_t[where], weighted, NT, preferred_element_type=jnp.float32)
+
+    give = sender(back_send, back_recv)
+    returns = {}
+    routes = {
+        low + high: ((0, upper, relay.at[0, 1], low), (2, lower, relay.at[1, 1], high)),
+        low + high + 1: ((1, upper, relay.at[0, 2], low + 1), (3, lower, relay.at[1, 2], high + 1)),
+        high + 1: ((6, lower, direct.at[3], high + 1), (4, upper, relay.at[0, 0], 1)),
+        low + 1: ((7, upper, direct.at[1], low + 1), (5, lower, relay.at[1, 0], 1)),
+        low: ((8, upper, direct.at[0], low),),
+        high: ((9, lower, direct.at[2], high),),
+    }
+    for r, ways in routes.items():
+        value = partial_of(r)
+        back[r] = value.astype(jnp.bfloat16)
+        if r == low:
+            kept[1] = value[half:]
+        if r == high:
+            kept[0] = value[:half]
+        for n, side, target, over in ways:
+            returns[n] = give(n, back.at[r, side], target, over)
+    back[1] = partial_of(1).astype(jnp.bfloat16)
+    returns[10] = give(10, back.at[1], mate_back, 1)
+    value = partial_of(0)
+    number, taken = number_of(brick, brick)
+    for k in range(own):
+        out_ref[k] = jnp.where((taken == 1) & (number == k), value, 0.0)
+
+    for n in range(6):
+        returns[n].wait_recv()
+    first = 11
+    for k in range(own):
+        for side, via, other in ((0, high, low), (1, low, high)):
+            total = jnp.zeros((half, width), jnp.float32)
+            for n, r in enumerate((0, 1, other, other + 1)):
+                number, taken = number_of(partner(r) if r else brick, partner(via))
+                value = relay[side, n - 1].astype(jnp.float32) if n else kept[side]
+                total = total + jnp.where((taken == 1) & (number == k), value, 0.0)
+            sums[side, k] = total.astype(jnp.bfloat16)
+            n = first + 2 * k + side
+            returns[n] = give(n, sums.at[side, k], sums_back.at[side, k], via)
+
+    for n in range(6, first):
+        returns[n].wait_recv()
+    for side, rows, other in ((0, upper, low), (1, lower, high)):
+        pieces = []
+        for r in (1, other, other + 1):
+            number, taken = number_of(partner(r), brick)
+            value = mate_back[rows] if r == 1 else direct[2 * side + r - other]
+            pieces.append((number, taken, value.astype(jnp.float32)))
+        for k in range(own):
+            total = out_ref[k, rows]
+            for number, taken, value in pieces:
+                total = total + jnp.where((taken == 1) & (number == k), value, 0.0)
+            out_ref[k, rows] = total
+    for k in range(own):
+        for side, rows in ((0, upper), (1, lower)):
+            returns[first + 2 * k + side].wait_recv()
+            out_ref[k, rows] = out_ref[k, rows] + sums_back[side, k].astype(jnp.float32)
+    for n in returns:
+        returns[n].wait_send()
+
+
+def cube_call(groups, bricks, store, crossing, phi, rows_index, cols_index):
+    own, width = store.shape[0], store.shape[1]
+    blocks = crossing.shape[0]
+    size_x, size_y, size_z, functions = phi.shape
+    points = size_x * size_y * size_z
+    tall, wide = size_x, size_y * size_z
+    half = width // 2
+    hbm = pl.BlockSpec(memory_space=pl.ANY)
+    tables = (blocks, width, points)
+    back_copies = 11 + 2 * own
+    return pl.pallas_call(
+        functools.partial(cube_kernel, groups, bricks, size_z),
+        out_shape=jax.ShapeDtypeStruct((own, width, width), jnp.float32),
+        in_specs=[pl.BlockSpec(memory_space=pltpu.SMEM), hbm, hbm, hbm, hbm],
+        out_specs=pl.BlockSpec(memory_space=pltpu.VMEM),
+        scratch_shapes=[
+            pltpu.VMEM(rows_index.shape, jnp.int32),
+            pltpu.VMEM(cols_index.shape, jnp.int32),
+            pltpu.VMEM((own, width, width), jnp.bfloat16),
+            pltpu.VMEM((points, functions), jnp.bfloat16),
+            pltpu.VMEM((width, width), jnp.bfloat16),
+            pltpu.VMEM((10, half, width), jnp.bfloat16),
+            pltpu.VMEM((2, own, half, width), jnp.bfloat16),
+            pltpu.VMEM((bricks, width, width), jnp.bfloat16),
+            pltpu.VMEM(tables, jnp.bfloat16),
+            pltpu.VMEM(tables, jnp.bfloat16),
+            pltpu.VMEM((tall, wide), jnp.float32),
+            pltpu.VMEM((3, 3, tall, wide), jnp.float32),
+            pltpu.VMEM((bricks, width, width), jnp.bfloat16),
+            pltpu.VMEM((2, half, width), jnp.float32),
+            pltpu.VMEM((2, 3, half, width), jnp.bfloat16),
+            pltpu.VMEM((2, own, half, width), jnp.bfloat16),
+            pltpu.VMEM((4, half, width), jnp.bfloat16),
+            pltpu.VMEM((width, width), jnp.bfloat16),
+            pltpu.VMEM((2, own, half, width), jnp.bfloat16),
+            pltpu.SemaphoreType.DMA((4,)),
+            pltpu.SemaphoreType.DMA((13,)),
+            pltpu.SemaphoreType.DMA((13,)),
+            pltpu.SemaphoreType.REGULAR((groups,)),
+            pltpu.SemaphoreType.DMA((8,)),
+            pltpu.SemaphoreType.DMA((8,)),
+            pltpu.SemaphoreType.DMA((back_copies,)),
+            pltpu.SemaphoreType.DMA((back_copies,)),
+        ],
+        compiler_params=pltpu.CompilerParams(
+            collective_id=0, has_side_effects=True, vmem_limit_bytes=60 << 20
+        ),
+    )(crossing, rows_index, cols_index, store, phi.reshape(points, functions))
+
+
 def local(groups, bricks, store, crossing, phi, rows_index, cols_index):
     own, width = store.shape[0], store.shape[1]
     crossing = crossing.T
@@ -208,6 +482,8 @@
     points = size_x * size_y * size_z
     tall, wide = size_x, size_y * size_z
     slots = (bricks, width, width)
+    if bricks == CORE * LOW * HIGH:
+        return cube_call(groups, bricks, store, crossing, phi, rows_index, cols_index)
     return pl.pallas_call(
         functools.partial(kernel, groups, bricks, size_z),
         out_shape=jax.ShapeDtypeStruct((own, width, width), jnp.float32),

time: 41.5 us -> 38.2 us (0.920)
  Pallas kernels: 39.1 us -> 36 us
    pallas_call x1, Pallas kernels: 39.1 us -> 36 us  [cube_call(): pl.pallas_call(functools.partial(cube_kernel, groups, bricks, size_z), ou...]
where the time goes in v1:
time: 38.2 us; the launch traced here: 38.1 us
  Pallas kernels  36 us (94%)
  local copies, waits for them, and re-layouts  2.06 us (5%)
    pallas_call x1, Pallas kernels, cube_call(): pl.pallas_call(functools.partial(cube_kernel, groups, bricks, size_z), ou...  36 us
    unnamed x1, local copies, waits for them, and re-layouts  2.06 us

profile of v1, /device:TPU:0, one launch (start us, length us, event | category | flops | bytes accessed | tf_op | source)
XLA Modules:
  0.0 38.1 jit_solution(15003908968546071724)
XLA Ops:
  0.0 36.0 %shard_map.55 = f32[3,256,256]{2,1,0:T(8,128)} custom-call(s32[4,8]{1,0:T(4,128)} %bitcast.3, s32[1,4,256]{2,1,0:T(4,128)} %rows_hbm.1, s32[1,4,256]{2,1,0:T(4,128)} %cols_hbm.1, bf16[3,256,256]{2,1,0:T(8,128)(2,1)} %store_hbm.1, bf16[1024,1024]{1,0:T(8,128)(2,1)} %bitcast.2), custom_call_target="tpu_custom_call" | custom-call | tf_op jit(solution)/shard_map/pallas_call | solution.py:437
  36.0 2.1 %copy.7 = f32[3,256,256]{2,1,0:T(8,128)} copy(f32[3,256,256]{2,1,0:T(8,128)} %shard_map.55) | data formatting | bytes 1572864

commit v2 on v1

--- a/solution.py
+++ b/solution.py
@@ -219,10 +219,10 @@
 
 def cube_kernel(
     groups, bricks, size_z,
-    crossing_ref, rows_hbm, cols_hbm, store_hbm, phi_hbm, out_ref,
+    crossing_ref, rows_hbm, cols_hbm, store_hbm, phi_hbm, near_hbm, far_hbm,
     rows_ref, cols_ref, store_v, phi_v, mate, picked, stage, incoming, row_t, col_t,
-    dens, halo, back, kept, relay, sums, direct, mate_back, sums_back,
-    load_sem, send_sem, recv_sem, ready, halo_send, halo_recv, back_send, back_recv,
+    dens, halo, back, kept, relay, sums, direct, mate_back, total_v,
+    load_sem, near_sem, send_sem, recv_sem, ready, halo_send, halo_recv, back_send, back_recv,
 ):
     group = lax.axis_index("grp")
     brick = lax.axis_index("brick")
@@ -304,14 +304,17 @@
     for load in loads[1:]:
         load.wait()
     tabulate = make_tabulate(rows_ref, cols_ref, phi_v, row_t, col_t)
-    lax.fori_loop(0, blocks, tabulate, 0)
+    lax.fori_loop(0, blocks // 2, tabulate, 0)
+    spread(0)
+    lax.fori_loop(blocks // 2, blocks, tabulate, 0)
+    spread(1)
 
     sends[0].wait_recv()
     sends[1].wait_recv()
     relays = (
+        (11, 1, high, upper), (12, 1, low, lower),
         (7, low, high, upper), (9, high, low, lower),
         (8, low + 1, high, upper), (10, high + 1, low, lower),
-        (11, 1, high, upper), (12, 1, low, lower),
     )
     for n, r, via, side in relays:
         number, _ = number_of(partner(r), partner(via))
@@ -335,8 +338,8 @@
         term = jnp.sum(row_t[where].astype(jnp.float32) * product, axis=0, keepdims=True)
         density = density + jnp.where(taken == 1, term, 0.0)
         if step < len(arrivals) - 1:
-            spread(step)
-    for n in range(len(arrivals) - 1, groups):
+            spread(step + 2)
+    for n in range(len(arrivals) + 1, groups):
         spread(n)
     for x in range(tall):
         dens[x : x + 1, :] = density[:, x * wide : (x + 1) * wide]
@@ -387,7 +390,7 @@
     value = partial_of(0)
     number, taken = number_of(brick, brick)
     for k in range(own):
-        out_ref[k] = jnp.where((taken == 1) & (number == k), value, 0.0)
+        total_v[k] = jnp.where((taken == 1) & (number == k), value, 0.0)
 
     for n in range(6):
         returns[n].wait_recv()
@@ -401,7 +404,7 @@
                 total = total + jnp.where((taken == 1) & (number == k), value, 0.0)
             sums[side, k] = total.astype(jnp.bfloat16)
             n = first + 2 * k + side
-            returns[n] = give(n, sums.at[side, k], sums_back.at[side, k], via)
+            returns[n] = give(n, sums.at[side, k], far_hbm.at[k, upper if side == 0 else lower], via)
 
     for n in range(6, first):
         returns[n].wait_recv()
@@ -412,14 +415,15 @@
             value = mate_back[rows] if r == 1 else direct[2 * side + r - other]
             pieces.append((number, taken, value.astype(jnp.float32)))
         for k in range(own):
-            total = out_ref[k, rows]
+            total = total_v[k, rows]
             for number, taken, value in pieces:
                 total = total + jnp.where((taken == 1) & (number == k), value, 0.0)
-            out_ref[k, rows] = total
-    for k in range(own):
-        for side, rows in ((0, upper), (1, lower)):
-            returns[first + 2 * k + side].wait_recv()
-            out_ref[k, rows] = out_ref[k, rows] + sums_back[side, k].astype(jnp.float32)
+            total_v[k, rows] = total
+    keep = pltpu.make_async_copy(total_v, near_hbm, near_sem)
+    keep.start()
+    keep.wait()
+    for n in range(first, first + 2 * own):
+        returns[n].wait_recv()
     for n in returns:
         returns[n].wait_send()
 
@@ -434,11 +438,14 @@
     hbm = pl.BlockSpec(memory_space=pl.ANY)
     tables = (blocks, width, points)
     back_copies = 11 + 2 * own
-    return pl.pallas_call(
+    near, far = pl.pallas_call(
         functools.partial(cube_kernel, groups, bricks, size_z),
-        out_shape=jax.ShapeDtypeStruct((own, width, width), jnp.float32),
+        out_shape=[
+            jax.ShapeDtypeStruct((own, width, width), jnp.float32),
+            jax.ShapeDtypeStruct((own, width, width), jnp.bfloat16),
+        ],
         in_specs=[pl.BlockSpec(memory_space=pltpu.SMEM), hbm, hbm, hbm, hbm],
-        out_specs=pl.BlockSpec(memory_space=pltpu.VMEM),
+        out_specs=[hbm, hbm],
         scratch_shapes=[
             pltpu.VMEM(rows_index.shape, jnp.int32),
             pltpu.VMEM(cols_index.shape, jnp.int32),
@@ -458,8 +465,9 @@
             pltpu.VMEM((2, own, half, width), jnp.bfloat16),
             pltpu.VMEM((4, half, width), jnp.bfloat16),
             pltpu.VMEM((width, width), jnp.bfloat16),
-            pltpu.VMEM((2, own, half, width), jnp.bfloat16),
+            pltpu.VMEM((own, width, width), jnp.float32),
             pltpu.SemaphoreType.DMA((4,)),
+            pltpu.SemaphoreType.DMA,
             pltpu.SemaphoreType.DMA((13,)),
             pltpu.SemaphoreType.DMA((13,)),
             pltpu.SemaphoreType.REGULAR((groups,)),
@@ -472,6 +480,7 @@
             collective_id=0, has_side_effects=True, vmem_limit_bytes=60 << 20
         ),
     )(crossing, rows_index, cols_index, store, phi.reshape(points, functions))
+    return near + far.astype(jnp.float32)
 
 
 def local(groups, bricks, store, crossing, phi, rows_index, cols_index):

time: 38.2 us -> 37.5 us (0.982)
  other arithmetic: 0 us -> 2.19 us
  local copies, waits for them, and re-layouts: 2.06 us -> 0 us
  Pallas kernels: 36 us -> 35.1 us
    add x0 -> x1, other arithmetic: none -> 2.19 us  [cube_call(): return near + far.astype(jnp.float32)]
    unnamed x1 -> x0, local copies, waits for them, and re-layouts: 2.06 us -> none
    pallas_call x1, Pallas kernels: 36 us -> 35.1 us  [cube_call(): pl.pallas_call(functools.partial(cube_kernel, groups, bricks, size_z), ou...]
where the time goes in v2:
time: 37.5 us; the launch traced here: 37.3 us
  Pallas kernels  35.1 us (94%)
  other arithmetic  2.19 us (6%)
    pallas_call x1, Pallas kernels, cube_call(): pl.pallas_call(functools.partial(cube_kernel, groups, bricks, size_z), ou...  35.1 us
    add x1, other arithmetic, cube_call(): return near + far.astype(jnp.float32)  2.19 us

profile of v2, /device:TPU:0, one launch (start us, length us, event | category | flops | bytes accessed | tf_op | source)
XLA Modules:
  0.0 37.3 jit_solution(7189701248709747547)
XLA Ops:
  0.0 35.1 %shard_map.55 = (f32[3,256,256]{2,1,0:T(8,128)}, bf16[3,256,256]{2,1,0:T(8,128)(2,1)}) custom-call(s32[4,8]{1,0:T(4,128)} %bitcast.3, s32[1,4,256]{2,1,0:T(4,128)} %rows_hbm.1, s32[1,4,256]{2,1,0:T(4,128)} %cols_hbm.1, bf16[3,256,256]{2,1,0:T(8,128)(2,1)} %store_hbm.1, bf16[1024,1024]{1,0:T(8,128)(2,1)} %bitcast.2), custom_call_target="tpu_custom_call" | custom-call | tf_op jit(solution)/shard_map/pallas_call | solution.py:441
  35.1 2.2 %convert_add_fusion = f32[3,256,256]{2,1,0:T(8,128)} fusion(f32[3,256,256]{2,1,0:T(8,128)} %get-tuple-element.7, bf16[3,256,256]{2,1,0:T(8,128)(2,1)} %get-tuple-element.8), kind=kLoop, calls=%fused_computation | loop fusion | flops 393216 | bytes 1966080 | tf_op jit(solution)/shard_map/add | solution.py:483

commit v3 on v2

--- a/solution.py
+++ b/solution.py
@@ -264,6 +264,7 @@
     along_chain(barrier)
     for load in loads:
         load.start()
+    loads[0].wait()
     pl.semaphore_wait(barrier, len(near) + links)
 
     for r in near:
@@ -288,9 +289,8 @@
 
     give = sender(send_sem, recv_sem)
     sends = {}
-    sends[0] = give(0, store_hbm.at[:, upper], stage.at[0], high)
-    sends[1] = give(1, store_hbm.at[:, lower], stage.at[1], low)
-    loads[0].wait()
+    sends[0] = give(0, store_v.at[:, upper], stage.at[0], high)
+    sends[1] = give(1, store_v.at[:, lower], stage.at[1], low)
     for n, r, side in ((3, low, upper), (5, high, lower), (4, low + 1, upper), (6, high + 1, lower)):
         number, _ = number_of(partner(r), brick)
         picked[n - 3] = store_v[number, side]

time: 37.5 us -> 37.3 us (level)
  no operation moved by 1% of the time
where the time goes in v3:
time: 37.3 us; the launch traced here: 37.1 us
  Pallas kernels  34.9 us (94%)
  other arithmetic  2.19 us (6%)
    pallas_call x1, Pallas kernels, cube_call(): pl.pallas_call(functools.partial(cube_kernel, groups, bricks, size_z), ou...  34.9 us
    add x1, other arithmetic, cube_call(): return near + far.astype(jnp.float32)  2.19 us

profile of v3, /device:TPU:0, one launch (start us, length us, event | category | flops | bytes accessed | tf_op | source)
XLA Modules:
  0.0 37.1 jit_solution(15921870178954416270)
XLA Ops:
  0.0 34.9 %shard_map.55 = (f32[3,256,256]{2,1,0:T(8,128)}, bf16[3,256,256]{2,1,0:T(8,128)(2,1)}) custom-call(s32[4,8]{1,0:T(4,128)} %bitcast.3, s32[1,4,256]{2,1,0:T(4,128)} %rows_hbm.1, s32[1,4,256]{2,1,0:T(4,128)} %cols_hbm.1, bf16[3,256,256]{2,1,0:T(8,128)(2,1)} %store_hbm.1, bf16[1024,1024]{1,0:T(8,128)(2,1)} %bitcast.2), custom_call_target="tpu_custom_call" | custom-call | tf_op jit(solution)/shard_map/pallas_call | solution.py:441
  34.9 2.2 %convert_add_fusion = f32[3,256,256]{2,1,0:T(8,128)} fusion(f32[3,256,256]{2,1,0:T(8,128)} %get-tuple-element.7, bf16[3,256,256]{2,1,0:T(8,128)(2,1)} %get-tuple-element.8), kind=kLoop, calls=%fused_computation | loop fusion | flops 393216 | bytes 1966080 | tf_op jit(solution)/shard_map/add | solution.py:483
